TPU v7x, 256 devices: a whole 4x4x8 slice. The times are simulated.
256 devices in a mesh: group: 32 (over y, z), inner: 8 (over x, core).
Axes of the slice: x: 4, y: 4, z: 8, core: 2. Of those that a mesh axis runs over, the one named last changes fastest.
Arguments:
- tokens: bfloat16 [4096, 7168], P('group', 'inner'), may hold values from -6 to 6
- routes: int32 [4096, 4], P('group'), may hold values from 0 to 31, all different within a row; in each aligned block of 128 rows (0 to 127, 128 to 255, ...) at most 24 rows name the same one
- gate_weights: float32 [4096, 4], P('group'), may hold values from 0.1 to 1
- w_gate: bfloat16 [32, 7168, 2048], P('group', None, 'inner'), may hold values from -0.0625 to 0.0625
- w_up: bfloat16 [32, 7168, 2048], P('group', None, 'inner'), may hold values from -0.0625 to 0.0625
- w_down: bfloat16 [32, 2048, 7168], P('group', 'inner'), may hold values from -0.125 to 0.125
Outputs:
- moe_out: bfloat16 [4096, 7168], P('group', 'inner')
Inputs may be any that keep to these rules, and one draw needn't show every extreme that they name: `routes`: each row names 4 different expert groups. Within each aligned block of 128 rows (the rows of one index of group) no group is named by more than 24 rows, and in some blocks one group is named by exactly 24 rows.
All inputs are finite; a program needn't handle non-finite values.
Results may differ from a plain program's by a relative error of at most 0.014.
Values may be sent and summed in bfloat16 or wider, within the bound.
A program may use at most 128 MiB of HBM per device.

v0:
```python
import jax
import jax.numpy as jnp
from jax import lax
from jax.sharding import PartitionSpec as P


def layout(routes, groups, capacity):
    group_ids = jnp.arange(groups, dtype=jnp.int32)
    onehot = routes[:, :, None] == group_ids[None, None, :]
    chosen = jnp.sum(onehot.astype(jnp.int32), axis=1)
    slot_of = jnp.cumsum(chosen, axis=0) - 1
    slot_ids = jnp.arange(capacity, dtype=jnp.int32)
    placing = (chosen.T[:, None, :] == 1) & (slot_of.T[:, None, :] == slot_ids[None, :, None])
    pick_slot = jnp.take_along_axis(slot_of, routes, axis=1)
    pick_index = routes * capacity + pick_slot
    return (placing, pick_index)


def pack_rows(placing, token_rows):
    packed = jnp.einsum(
        "hct,td->hcd", placing.astype(jnp.bfloat16), token_rows, preferred_element_type=jnp.float32
    )
    return packed.astype(jnp.bfloat16)


def combine(pick_index, gate_weights, returned):
    flat_rows = returned.reshape(returned.shape[0] * returned.shape[1], returned.shape[2])
    taken = jnp.take(flat_rows, pick_index, axis=0).astype(jnp.float32)
    return jnp.sum(taken * gate_weights[:, :, None], axis=1)


def local(tokens, routes, gate_weights, w_gate, w_up, w_down):
    groups = lax.axis_size("group")
    shard_rows = tokens.shape[0]
    capacity = shard_rows * routes.shape[1] * 3 // (2 * groups)
    placing, pick_index = layout(routes, groups, capacity)
    gate_mat = w_gate[0]
    up_mat = w_up[0]
    down_mat = w_down[0]
    arrived = lax.all_to_all(
        pack_rows(placing, tokens), "group", split_axis=0, concat_axis=0, tiled=True
    )
    feature_part = lax.all_gather(arrived, "inner", axis=2, tiled=True)
    gate_add = jnp.einsum("hck,kf->hcf", feature_part, gate_mat, preferred_element_type=jnp.float32)
    up_add = jnp.einsum("hck,kf->hcf", feature_part, up_mat, preferred_element_type=jnp.float32)
    hidden = (jax.nn.silu(gate_add) * up_add).astype(jnp.bfloat16)
    partial_value = jnp.einsum(
        "hcf,fd->hcd", hidden, down_mat, preferred_element_type=jnp.float32
    ).astype(jnp.bfloat16)
    summed = lax.psum_scatter(partial_value, "inner", scatter_dimension=2, tiled=True)
    returned = lax.all_to_all(summed, "group", split_axis=0, concat_axis=0, tiled=True)
    return combine(pick_index, gate_weights, returned).astype(jnp.bfloat16)


def solution(mesh):
    placed = (
        P("group", "inner"),
        P("group", None),
        P("group", None),
        P("group", None, "inner"),
        P("group", None, "inner"),
        P("group", "inner", None),
    )
    return jax.shard_map(
        local, mesh=mesh, in_specs=placed, out_specs=P("group", "inner"), check_vma=False
    )
```

profile of v0, /device:TPU:32, one launch (start us, length us, event | category | flops | bytes accessed | tf_op | source)
XLA Modules:
  0.0 412.8 jit_solution(16734024208027349280)
XLA Ops:
  6.5 0.0 copy-start
  6.5 0.0 all-gather.2.cloned.1.call-start
  6.5 0.7 convert_reduce_fusion
  7.3 0.1 copy.44
  7.4 0.2 reduce_window_sum.11
  7.6 0.1 copy.48
  7.6 0.0 copy-done
  7.6 0.5 convolution_convert_fusion.1
  8.2 47.4 %all_to_all.10 = bf16[32,24,896]{2,1,0:T(8,128)(2,1)} all-to-all(bf16[32,24,896]{2,1,0:T(8,128)(2,1)S(1)} %convolution_convert_fusion.1), channel_id=1, replica_groups=mesh['group'=32,'inner'=8] {'group'}, dimensions={0} | all-to-all | bytes 2752512 | tf_op jit(solution)/shard_map/all_to_all | solution.py:40
  55.6 0.0 all-gather.2.cloned.1.call-update
  55.6 0.0 reduce-scatter.4.cloned.1.call-start
  55.6 59.1 %all-gather.2.cloned.1.call-done = bf16[32,24,7168]{2,1,0:T(8,128)(2,1)} async-done(((bf16[32,24,896]{2,1,0:T(8,128)(2,1)}), bf16[32,24,7168]{2,1,0:T(8,128)(2,1)}) %all-gather.2.cloned.1.call-update) | async-done | bytes 11010064 | tf_op jit(solution)/shard_map/all_gather | solution.py:43
  114.7 0.0 copy-start.5
  114.7 0.0 copy-start.6
  114.7 7.0 %fusion.3 = f32[32,24,256]{2,1,0:T(8,128)S(1)} fusion(bf16[32,24,7168]{2,1,0:T(8,128)(2,1)} %all-gather.2.cloned.1.call-done, bf16[1,7168,256]{2,1,0:T(8,128)(2,1)} %param.9), kind=kOutput, calls=%fused_computation.6 | convolution fusion | flops 2818572288 | bytes 15466496 | tf_op jit(solution)/shard_map/hck,kf->hcf/dot_general | solution.py:44
  121.8 1.3 copy-done.5
  123.1 1.0 copy-done.6
  124.1 0.0 copy-start.2
  124.1 3.2 fusion.8
  127.4 0.0 copy-done.2
  127.4 5.8 %convolution_convert_fusion = bf16[32,24,7168]{2,1,0:T(8,128)(2,1)} fusion(bf16[32,24,256]{2,1,0:T(8,128)(2,1)S(1)} %fusion.8, bf16[1,256,7168]{2,1,0:T(8,128)(2,1)S(1)} %copy-done.2), kind=kOutput, calls=%fused_computation.2 | convolution fusion | flops 2824077312 | bytes 15073280 | tf_op jit(solution)/shard_map/hcf,fd->hcd/dot_general | solution.py:47
  133.2 51.3 %copy.51 = bf16[32,24,7168]{1,0,2:T(8,128)(2,1)} copy(bf16[32,24,7168]{2,1,0:T(8,128)(2,1)} %convolution_convert_fusion) | data formatting | bytes 22020096
  184.5 81.1 %reshape.49 = bf16[7168,768]{1,0:T(8,128)(2,1)} reshape(bf16[7168,32,24]{2,1,0:T(8,128)(2,1)} %bitcast.33) | data formatting | bytes 22020096
  265.6 0.0 reduce-scatter.4.cloned.1.call-update
  265.6 68.0 %reduce-scatter.4.cloned.1.call-done = bf16[896,768]{1,0:T(8,128)(2,1)} async-done(((bf16[7168,768]{1,0:T(8,128)(2,1)}), bf16[896,768]{1,0:T(8,128)(2,1)}) %reduce-scatter.4.cloned.1.call-update) | async-done | bytes 1376272
  333.7 13.4 %reshape.50 = bf16[896,32,24]{2,1,0:T(8,128)(2,1)} reshape(bf16[896,768]{1,0:T(8,128)(2,1)} %reduce-scatter.4.cloned.1.call-done) | data formatting | bytes 2752512
  347.0 0.0 copy-start.3
  347.0 9.7 %copy.52 = bf16[32,24,896]{2,1,0:T(8,128)(2,1)} copy(bf16[32,24,896]{1,0,2:T(8,128)(2,1)} %bitcast.35) | data formatting | bytes 2752512
  356.8 10.1 %all-to-all-start.1 = ((bf16[32,24,896]{2,1,0:T(8,128)(2,1)}), bf16[32,24,896]{2,1,0:T(8,128)(2,1)S(1)}, u32[]{:S(2)}, u32[]{:S(2)}) async-start(bf16[32,24,896]{2,1,0:T(8,128)(2,1)} %copy.52), calls=%async_computation.1 | async-start | bytes 2752512 | tf_op jit(solution)/shard_map/all_to_all | solution.py:51
  366.9 0.0 copy-done.3
  366.9 0.1 copy.45
  367.0 0.1 reshape.32
  367.1 0.0 copy-start.4
  367.1 3.8 gather_fusion.1
  370.9 0.1 reshape.35
  371.0 0.1 copy.46
  371.1 0.1 copy.49
  371.2 0.1 reshape.26
  371.3 0.1 copy.47
  371.5 0.0 copy-done.4
  371.5 0.1 copy.50
  371.6 30.0 %all-to-all-done.1 = bf16[32,24,896]{2,1,0:T(8,128)(2,1)S(1)} async-done(((bf16[32,24,896]{2,1,0:T(8,128)(2,1)}), bf16[32,24,896]{2,1,0:T(8,128)(2,1)S(1)}, u32[]{:S(2)}, u32[]{:S(2)}) %all-to-all-start.1) | async-done | bytes 1376288 | tf_op jit(solution)/shard_map/all_to_all | solution.py:51
  401.6 0.0 copy-start.1
  401.6 2.0 gather_fusion
  403.6 0.2 reshape.25
  403.9 2.1 multiply_reduce_fusion
  406.0 0.0 copy-done.1
  (5 shorter events, 0.1 us)
Async XLA Ops:
  6.5 1.1 copy-start
  6.5 108.2 %all-gather.2.cloned.1.call-start = ((), (), s32[]{:S(2)}) async-start(), calls=%async_computation.3 | async-start | bytes 12386304 | tf_op jit(solution)/shard_map/all_gather | solution.py:43
  55.6 278.1 %reduce-scatter.4.cloned.1.call-start = ((), (), s32[]{:S(2)}) async-start(), calls=%async_computation.4 | async-start | bytes 12386304
  114.7 8.4 %copy-start.5 = (bf16[32,24,7168]{2,1,0:T(8,128)(2,1)S(1)}, bf16[32,24,7168]{2,1,0:T(8,128)(2,1)}, u32[]{:S(2)}) copy-start(bf16[32,24,7168]{2,1,0:T(8,128)(2,1)} %all-gather.2.cloned.1.call-done) | copy-start | bytes 33030148
  114.7 9.4 %copy-start.6 = (bf16[1,7168,256]{2,1,0:T(8,128)(2,1)S(1)}, bf16[1,7168,256]{2,1,0:T(8,128)(2,1)}, u32[]{:S(2)}) copy-start(bf16[1,7168,256]{2,1,0:T(8,128)(2,1)} %param.10) | copy-start | bytes 11010052
  124.1 3.2 copy-start.2
  347.0 19.8 %copy-start.3 = (s32[128,4]{0,1:T(4,128)S(1)}, s32[128,4]{0,1:T(4,128)}, u32[]{:S(2)}) copy-start(s32[128,4]{0,1:T(4,128)} %param.7) | copy-start | bytes 6148
  356.8 44.8 %all-to-all-start.1 = ((bf16[32,24,896]{2,1,0:T(8,128)(2,1)}), bf16[32,24,896]{2,1,0:T(8,128)(2,1)S(1)}, u32[]{:S(2)}, u32[]{:S(2)}) async-start(bf16[32,24,896]{2,1,0:T(8,128)(2,1)} %copy.52), calls=%async_computation.1 | async-start | bytes 2752512 | tf_op jit(solution)/shard_map/all_to_all | solution.py:51
  367.1 4.4 %copy-start.4 = (f32[128,4]{0,1:T(4,128)S(1)}, f32[128,4]{0,1:T(4,128)}, u32[]{:S(2)}) copy-start(f32[128,4]{0,1:T(4,128)} %param.8) | copy-start | bytes 6148
  401.6 4.4 %copy-start.1 = (bf16[128,896]{1,0:T(8,128)(2,1)S(1)}, bf16[128,896]{1,0:T(8,128)(2,1)}, u32[]{:S(2)}) copy-start(bf16[128,896]{1,0:T(8,128)(2,1)} %param.6) | copy-start | bytes 688132
Sparse Core Ops, SparseCore 0:
  55.7 58.9 all-gather.1
  265.8 67.8 reduce-scatter.3
where the time goes:
time: 417 us; the launch traced here: 413 us
  local copies, waits for them, and re-layouts  165 us (40%)
  waiting for transfers between devices  157 us (38%)
  blocking collectives  47.4 us (11%)
  matrix products  16.6 us (4%)
  between operations  13.5 us (3%)
  starting transfers between devices  10.1 us (2%)
    unnamed x19, local copies, waits for them, and re-layouts  158 us
    unnamed x3, waiting for transfers between devices  68 us
    all_gather x1, waiting for transfers between devices, local(): feature_part = lax.all_gather(arrived, 'inner', axis=2, tiled=True)  59.1 us
    all_to_all x1, blocking collectives, local(): lax.all_to_all(pack_rows(placing, tokens), 'group', split_axis=0, concat_...  47.4 us
    all_to_all x1, waiting for transfers between devices, local(): lax.all_to_all(summed, 'group', split_axis=0, concat_axis=0, tiled=True)  30 us
    all_to_all x1, starting transfers between devices, local(): lax.all_to_all(summed, 'group', split_axis=0, concat_axis=0, tiled=True)  10.1 us
  transfers between devices with their start and end apart: 3, of which 3 were waited for; matrix products, arithmetic and copies ran while one was open for 1% of the time, Pallas kernels for 0%

commit v1 on v0

--- a/solution.py
+++ b/solution.py
@@ -40,7 +40,19 @@
     arrived = lax.all_to_all(
         pack_rows(placing, tokens), "group", split_axis=0, concat_axis=0, tiled=True
     )
-    feature_part = lax.all_gather(arrived, "inner", axis=2, tiled=True)
+
+    def derive_matrix(in_dim, local_block, named_axis):
+        return jnp.concatenate(
+            lax.all_to_all(
+                jnp.stack([local_block] * lax.axis_size(named_axis), axis=0),
+                axis_name=named_axis,
+                split_axis=0,
+                concat_axis=0,
+            ),
+            in_dim,
+        )
+
+    feature_part = derive_matrix(2, arrived, "inner")
     gate_add = jnp.einsum("hck,kf->hcf", feature_part, gate_mat, preferred_element_type=jnp.float32)
     up_add = jnp.einsum("hck,kf->hcf", feature_part, up_mat, preferred_element_type=jnp.float32)
     hidden = (jax.nn.silu(gate_add) * up_add).astype(jnp.bfloat16)

time: 417 us -> 481 us (1.15)
  blocking collectives: 47.4 us -> 174 us
  waiting for transfers between devices: 157 us -> 92.6 us
  local copies, waits for them, and re-layouts: 165 us -> 171 us
    all_to_all x0 -> x1, blocking collectives: none -> 127 us  [derive_matrix(): lax.all_to_all(jnp.stack([local_block] * lax.axis_size(named_axis), axis=...]
    all_gather x1 -> x0, waiting for transfers between devices: 59.1 us -> none  [local(): feature_part = lax.all_gather(arrived, 'inner', axis=2, tiled=True)]
    unnamed x3 -> x2, waiting for transfers between devices: 68 us -> 62.6 us
    another operation x0 -> x1, local copies, waits for them, and re-layouts: none -> 5.01 us  [derive_matrix(): jnp.stack([local_block] * lax.axis_size(named_axis), axis=0)]
  transfers between devices with their start and end apart: 3 -> 2, of which waited for: 3 -> 2; matrix products, arithmetic and copies ran while one was open for 1% -> 1% of each run, Pallas kernels for 0% -> 0%
where the time goes in v1:
time: 481 us; the launch traced here: 477 us
  blocking collectives  174 us (36%)
  local copies, waits for them, and re-layouts  171 us (36%)
  waiting for transfers between devices  92.6 us (19%)
  between operations  13.6 us (3%)
  matrix products  12.8 us (3%)
  starting transfers between devices  10.1 us (2%)
    unnamed x19, local copies, waits for them, and re-layouts  156 us
    all_to_all x1, blocking collectives, derive_matrix(): lax.all_to_all(jnp.stack([local_block] * lax.axis_size(named_axis), axis=...  127 us
    unnamed x2, waiting for transfers between devices  62.6 us
    all_to_all x1, blocking collectives, local(): lax.all_to_all(pack_rows(placing, tokens), 'group', split_axis=0, concat_...  47.3 us
    all_to_all x1, waiting for transfers between devices, local(): lax.all_to_all(summed, 'group', split_axis=0, concat_axis=0, tiled=True)  30 us
    all_to_all x1, starting transfers between devices, local(): lax.all_to_all(summed, 'group', split_axis=0, concat_axis=0, tiled=True)  10.1 us
  transfers between devices with their start and end apart: 2, of which 2 were waited for; matrix products, arithmetic and copies ran while one was open for 1% of the time, Pallas kernels for 0%

profile of v1, /device:TPU:32, one launch (start us, length us, event | category | flops | bytes accessed | tf_op | source)
XLA Modules:
  0.0 477.2 jit_solution(18128222939110414743)
XLA Ops:
  6.5 0.0 copy-start
  6.5 0.0 reduce-scatter.4.cloned.1.call-start
  6.5 0.7 convert_reduce_fusion
  7.3 0.1 copy.46
  7.4 0.2 reduce_window_sum.11
  7.6 0.1 copy.50
  7.6 0.0 copy-done
  7.6 0.5 convolution_convert_fusion.1
  8.2 47.3 %all_to_all.15 = bf16[32,24,896]{2,1,0:T(8,128)(2,1)S(1)} all-to-all(bf16[32,24,896]{2,1,0:T(8,128)(2,1)S(1)} %convolution_convert_fusion.1), channel_id=1, replica_groups=mesh['group'=32,'inner'=8] {'group'}, dimensions={0} | all-to-all | bytes 2752512 | tf_op jit(solution)/shard_map/all_to_all | solution.py:40
  55.4 5.0 %stack.2 = bf16[8,32,24,896]{3,2,1,0:T(8,128)(2,1)} broadcast(bf16[32,24,896]{2,1,0:T(8,128)(2,1)S(1)} %all_to_all.15), dimensions={1,2,3} | broadcast | bytes 12386304 | tf_op jit(solution)/shard_map/stack | solution.py:47
  60.5 127.0 %all_to_all.16 = bf16[8,32,24,896]{3,2,1,0:T(8,128)(2,1)S(1)} all-to-all(bf16[8,32,24,896]{3,2,1,0:T(8,128)(2,1)} %stack.2), channel_id=1, replica_groups=mesh['group'=32,'inner'=8] {'inner'}, dimensions={0} | all-to-all | bytes 22020096 | tf_op jit(solution)/shard_map/all_to_all | solution.py:46
  187.5 0.0 copy-start.5
  187.5 3.3 copy.56
  190.8 0.0 copy-done.5
  190.8 0.0 copy-start.6
  190.8 3.2 fusion.3
  194.0 0.0 copy-done.6
  194.0 0.0 copy-start.2
  194.1 3.3 fusion.8
  197.4 0.0 copy-done.2
  197.4 5.7 %convolution_convert_fusion = bf16[32,24,7168]{2,1,0:T(8,128)(2,1)} fusion(bf16[32,24,256]{2,1,0:T(8,128)(2,1)S(1)} %fusion.8, bf16[1,256,7168]{2,1,0:T(8,128)(2,1)S(1)} %copy-done.2), kind=kOutput, calls=%fused_computation.2 | convolution fusion | flops 2824077312 | bytes 15073280 | tf_op jit(solution)/shard_map/hcf,fd->hcd/dot_general | solution.py:59
  203.1 51.2 %copy.54 = bf16[32,24,7168]{1,0,2:T(8,128)(2,1)} copy(bf16[32,24,7168]{2,1,0:T(8,128)(2,1)} %convolution_convert_fusion) | data formatting | bytes 22020096
  254.3 81.1 %reshape.59 = bf16[7168,768]{1,0:T(8,128)(2,1)} reshape(bf16[7168,32,24]{2,1,0:T(8,128)(2,1)} %bitcast.36) | data formatting | bytes 22020096
  335.4 0.0 reduce-scatter.4.cloned.1.call-update
  335.4 62.5 %reduce-scatter.4.cloned.1.call-done = bf16[896,768]{1,0:T(8,128)(2,1)} async-done(((bf16[7168,768]{1,0:T(8,128)(2,1)}), bf16[896,768]{1,0:T(8,128)(2,1)}) %reduce-scatter.4.cloned.1.call-update) | async-done | bytes 1376272
  398.0 13.4 %reshape.60 = bf16[896,32,24]{2,1,0:T(8,128)(2,1)} reshape(bf16[896,768]{1,0:T(8,128)(2,1)} %reduce-scatter.4.cloned.1.call-done) | data formatting | bytes 2752512
  411.4 0.0 copy-start.3
  411.4 9.8 %copy.55 = bf16[32,24,896]{2,1,0:T(8,128)(2,1)} copy(bf16[32,24,896]{1,0,2:T(8,128)(2,1)} %bitcast.39) | data formatting | bytes 2752512
  421.1 10.1 %all-to-all-start.2 = ((bf16[32,24,896]{2,1,0:T(8,128)(2,1)}), bf16[32,24,896]{2,1,0:T(8,128)(2,1)S(1)}, u32[]{:S(2)}, u32[]{:S(2)}) async-start(bf16[32,24,896]{2,1,0:T(8,128)(2,1)} %copy.55), calls=%async_computation.2 | async-start | bytes 2752512 | tf_op jit(solution)/shard_map/all_to_all | solution.py:63
  431.2 0.0 copy-done.3
  431.3 0.1 copy.47
  431.4 0.1 reshape.42
  431.5 0.0 copy-start.4
  431.5 3.8 gather_fusion.1
  435.3 0.1 reshape.45
  435.4 0.1 copy.48
  435.5 0.1 copy.52
  435.6 0.1 reshape.36
  435.7 0.1 copy.49
  435.8 0.0 copy-done.4
  435.8 0.1 copy.53
  436.0 30.0 %all-to-all-done.2 = bf16[32,24,896]{2,1,0:T(8,128)(2,1)S(1)} async-done(((bf16[32,24,896]{2,1,0:T(8,128)(2,1)}), bf16[32,24,896]{2,1,0:T(8,128)(2,1)S(1)}, u32[]{:S(2)}, u32[]{:S(2)}) %all-to-all-start.2) | async-done | bytes 1376288 | tf_op jit(solution)/shard_map/all_to_all | solution.py:63
  466.0 0.0 copy-start.1
  466.0 2.0 gather_fusion
  468.0 0.2 reshape.35
  468.2 2.1 multiply_reduce_fusion
  470.4 0.0 copy-done.1
  (5 shorter events, 0.1 us)
Async XLA Ops:
  6.5 1.1 copy-start
  6.5 391.4 %reduce-scatter.4.cloned.1.call-start = ((), (), s32[]{:S(2)}) async-start(), calls=%async_computation.4 | async-start | bytes 12386304
  187.5 3.3 copy-start.5
  190.8 3.2 copy-start.6
  194.0 3.3 copy-start.2
  411.4 19.9 %copy-start.3 = (s32[128,4]{0,1:T(4,128)S(1)}, s32[128,4]{0,1:T(4,128)}, u32[]{:S(2)}) copy-start(s32[128,4]{0,1:T(4,128)} %param.7) | copy-start | bytes 6148
  421.1 44.8 %all-to-all-start.2 = ((bf16[32,24,896]{2,1,0:T(8,128)(2,1)}), bf16[32,24,896]{2,1,0:T(8,128)(2,1)S(1)}, u32[]{:S(2)}, u32[]{:S(2)}) async-start(bf16[32,24,896]{2,1,0:T(8,128)(2,1)} %copy.55), calls=%async_computation.2 | async-start | bytes 2752512 | tf_op jit(solution)/shard_map/all_to_all | solution.py:63
  431.5 4.4 copy-start.4
  466.0 4.4 copy-start.1
Sparse Core Ops, SparseCore 0:
  335.6 62.3 reduce-scatter.3
